TPU v7x, 256 devices: a whole 4x4x8 slice. The times are simulated.
256 devices in a mesh: row: 16 (over x_hi, z), col: 16 (over y, x_lo, core).
Axes of the slice: x: 4 (x_hi: 2, x_lo: 2; x = x_hi * 2 + x_lo), y: 4, z: 8, core: 2. Of those that a mesh axis runs over, the one named last changes fastest.
Arguments:
- node_feats: bfloat16 [65536, 256], P(('row', 'col')), may hold values from -6 to 6
- dest_grad: bfloat16 [16, 4096, 256], P('col', 'row'), may hold values from -6 to 6
- bases: bfloat16 [30, 256, 256], replicated, may hold values from -0.375 to 0.375
- coefs: bfloat16 [2000, 30], replicated, may hold values from -1 to 1
- src_ids: int32 [16, 16, 1024], P('row', 'col'), may hold values from 0 to 4095
- dst_ids: int32 [16, 16, 1024], P('row', 'col'), may hold values from 0 to 4095
- rel_ids: int32 [16, 16, 1024], P('row', 'col'), may hold values from 0 to 1999
- edge_norm: float32 [16, 16, 1024], P('row', 'col'), may hold values from 0.1 to 1
- block_fill: int32 [16, 16, 8], P('row', 'col'), may hold values from 0 to 128, as said below
Outputs:
- node_grad: bfloat16 [65536, 256], P(('row', 'col'))
- basis_grad: float32 [7680, 256], P(('row', 'col'))
- coef_grad: float32 [2000, 30], replicated
Inputs may be any that keep to these rules, and one draw needn't show every extreme that they name: `block_fill`: the first block of every device is full, and blocks after a device's last live block are empty.
All inputs are finite; a program needn't handle non-finite values.
Results may differ from a plain program's by a relative error of at most 0.0049.
Values may be sent and summed in bfloat16 or wider, within the bound.
A program may use at most 64 MiB of HBM per device.

v0:
```python
import jax
import jax.numpy as jnp
from jax import lax
from jax.sharding import PartitionSpec as P

EDGE_BLOCK = 128


def on_device(
    node_feats, dest_grad, bases, coefs, src_ids, dst_ids, rel_ids, edge_norm, block_fill
):
    col_count = lax.axis_size("col")
    source_rows = lax.all_gather(node_feats, "col", axis=0, tiled=True)
    target_rows = lax.all_gather(dest_grad[0], "row", axis=0, tiled=True)
    sources = src_ids.reshape(-1)
    targets = dst_ids.reshape(-1)
    relations = rel_ids.reshape(-1)
    fills = block_fill.reshape(-1)
    block_total = fills.shape[0]
    position = lax.broadcasted_iota(jnp.int32, (block_total, EDGE_BLOCK), 1)
    live_mask = (position < fills[:, None]).reshape(-1).astype(jnp.float32)
    weights = edge_norm.reshape(-1) * live_mask
    edge_total = sources.shape[0]
    edge_grad = (weights[:, None] * target_rows[targets].astype(jnp.float32)).astype(jnp.bfloat16)
    edge_rows = source_rows[sources]
    edge_coefs = coefs[relations]
    basis_count = bases.shape[0]
    width = bases.shape[1]
    vertex_count = source_rows.shape[0]
    relation_count = coefs.shape[0]
    block_span = 512
    node_part = jnp.zeros((vertex_count, width), jnp.float32)
    coef_part = jnp.zeros((relation_count, basis_count), jnp.float32)
    for offset in range(0, edge_total, block_span):
        grad_block = edge_grad[offset : offset + block_span]
        rows_block = edge_rows[offset : offset + block_span]
        coef_block = edge_coefs[offset : offset + block_span].astype(jnp.float32)
        backed = lax.dot_general(
            grad_block, bases, (((1,), (2,)), ((), ())), preferred_element_type=jnp.float32
        )
        per_edge = jnp.sum(coef_block[:, :, None] * backed, axis=1)
        inner = jnp.sum(backed * rows_block[:, None, :].astype(jnp.float32), axis=2)
        node_part = node_part + jax.ops.segment_sum(
            per_edge, sources[offset : offset + block_span], num_segments=vertex_count
        )
        coef_part = coef_part + jax.ops.segment_sum(
            inner, relations[offset : offset + block_span], num_segments=relation_count
        )
    node_grad = lax.psum_scatter(node_part, "col", scatter_dimension=0, tiled=True).astype(
        jnp.bfloat16
    )
    basis_rows = (edge_coefs[:, :, None] * edge_rows[:, None, :]).reshape(
        edge_total, basis_count * width
    )
    basis_grad = lax.psum_scatter(
        lax.dot_general(
            basis_rows, edge_grad, (((0,), (0,)), ((), ())), preferred_element_type=jnp.float32
        ),
        ("row", "col"),
        scatter_dimension=0,
        tiled=True,
    )
    coef_grad = lax.psum(coef_part, ("row", "col"))
    return (node_grad, basis_grad / col_count, coef_grad / col_count)


def solution(mesh):
    in_specs = (
        P(("row", "col"), None),
        P("col", "row", None),
        P(),
        P(),
        P("row", "col", None),
        P("row", "col", None),
        P("row", "col", None),
        P("row", "col", None),
        P("row", "col", None),
    )
    out_specs = (P(("row", "col"), None), P(("row", "col"), None), P())
    return jax.shard_map(
        on_device, mesh=mesh, in_specs=in_specs, out_specs=out_specs, check_vma=False
    )
```

profile of v0, /device:TPU:4, one launch (start us, length us, event | category | flops | bytes accessed | tf_op | source)
XLA Modules:
  0.0 924.1 jit_solution(12984734901086320531)
XLA Ops:
  7.2 0.0 all-gather.4.cloned.1.call-start
  7.2 0.7 all-gather.4.cloned.1.call-update
  7.9 0.0 all-gather.6.cloned.1.call-start
  7.9 0.7 all-gather.6.cloned.1.call-update
  8.6 0.0 all-reduce.4.cloned.1.call-start
  8.7 1.2 copy.35
  9.9 0.7 compare_select_fusion.2
  10.6 3.2 gather_fusion
  13.8 0.2 copy.36
  14.0 0.7 slice_bitcast_fusion.7
  14.7 0.7 slice_bitcast_fusion.5
  15.4 0.7 compare_select_fusion
  16.1 0.7 compare_select_fusion.1
  16.8 0.8 fusion.8
  17.6 31.2 %all-gather.4.cloned.1.call-done = bf16[4096,256]{1,0:T(8,128)(2,1)} async-done(((bf16[256,256]{1,0:T(8,128)(2,1)}), bf16[4096,256]{1,0:T(8,128)(2,1)}) %all-gather.4.cloned.1.call-update) | async-done | bytes 2097168 | tf_op jit(solution)/shard_map/all_gather | solution.py:13
  48.8 5.3 gather_fusion.2
  54.1 0.1 slice_convert_fusion.1
  54.2 0.2 copy.42
  54.4 0.2 copy.41
  54.6 80.1 %all-gather.6.cloned.1.call-done = bf16[1,4096,256]{2,1,0:T(8,128)(2,1)} async-done(((bf16[1,256,256]{2,1,0:T(8,128)(2,1)}), bf16[1,4096,256]{2,1,0:T(8,128)(2,1)}) %all-gather.6.cloned.1.call-update) | async-done | bytes 2097168 | tf_op jit(solution)/shard_map/all_gather | solution.py:14
  134.7 5.3 gather_fusion.1
  140.0 0.2 multiply_convert_fusion
  140.2 0.0 copy-start
  140.2 6.3 multiply_reduce_fusion
  146.5 4.2 multiply_reduce_fusion.1
  150.7 0.2 copy.43
  151.0 7.0 scatter_custom_fusion.1
  158.0 0.0 all-reduce.4.cloned.1.call-update
  158.0 0.0 reduce-scatter.4.cloned.1.call-start
  158.0 1.3 pad_maximum_fusion
  159.3 0.3 copy.38
  159.7 8.3 scatter_custom_fusion
  167.9 0.0 reduce-scatter.4.cloned.1.call-update
  168.0 0.2 copy.40
  168.2 4.1 broadcast_multiply_fusion
  172.3 6.7 fusion.9
  179.0 597.6 %fusion = f32[32,256]{1,0:T(8,128)S(1)} fusion(f32[7680,256]{1,0:T(8,128)} %fusion.9), kind=kCustom, calls=%all-reduce-scatter | all-reduce-scatter fusion | flops 2097153 | bytes 7897088
  776.6 1.9 collective-permute-start.15
  778.6 1.9 collective-permute-start.14
  780.5 1.9 collective-permute-start.13
  782.4 1.9 collective-permute-start.12
  784.3 1.9 collective-permute-start.11
  786.3 0.0 collective-permute-done.15
  786.3 6.7 collective-permute-start.10
  793.0 0.0 collective-permute-done.14
  793.0 8.1 collective-permute-start.9
  801.1 0.0 collective-permute-done.13
  801.1 1.9 collective-permute-start.8
  803.1 14.8 %collective-permute-start.7 = (f32[32,256]{1,0:T(8,128)S(1)}, f32[32,256]{1,0:T(8,128)S(1)}, u32[]{:S(2)}, u32[]{:S(2)}) collective-permute-start(f32[32,256]{1,0:T(8,128)S(1)} %fusion), channel_id=1, source_target_pairs={{0,8},{1,9},{2,10},{3,11},{4,12},{5,13},{6,14},{7,15},{8,16},{9,17... | collective-permute-start | bytes 98312
  817.9 27.8 %collective-permute-start.6 = (f32[32,256]{1,0:T(8,128)S(1)}, f32[32,256]{1,0:T(8,128)S(1)}, u32[]{:S(2)}, u32[]{:S(2)}) collective-permute-start(f32[32,256]{1,0:T(8,128)S(1)} %fusion), channel_id=1, source_target_pairs={{0,7},{1,8},{2,9},{3,10},{4,11},{5,12},{6,13},{7,14},{8,15},{9,16}... | collective-permute-start | bytes 98312
  845.8 24.3 %collective-permute-start.5 = (f32[32,256]{1,0:T(8,128)S(1)}, f32[32,256]{1,0:T(8,128)S(1)}, u32[]{:S(2)}, u32[]{:S(2)}) collective-permute-start(f32[32,256]{1,0:T(8,128)S(1)} %fusion), channel_id=1, source_target_pairs={{0,6},{1,7},{2,8},{3,9},{4,10},{5,11},{6,12},{7,13},{8,14},{9,15},... | collective-permute-start | bytes 98312
  870.1 17.0 %collective-permute-start.4 = (f32[32,256]{1,0:T(8,128)S(1)}, f32[32,256]{1,0:T(8,128)S(1)}, u32[]{:S(2)}, u32[]{:S(2)}) collective-permute-start(f32[32,256]{1,0:T(8,128)S(1)} %fusion), channel_id=1, source_target_pairs={{0,5},{1,6},{2,7},{3,8},{4,9},{5,10},{6,11},{7,12},{8,13},{9,14},{... | collective-permute-start | bytes 98312
  887.1 2.5 collective-permute-start.3
  889.6 8.7 collective-permute-start.2
  898.3 3.0 collective-permute-start.1
  901.4 1.9 collective-permute-start
  903.4 3.7 collective-permute-done.2
  907.1 1.3 collective-permute-done.1
  908.4 2.5 collective-permute-done
  910.9 2.1 concatenate.16
  913.0 0.6 dynamic-slice_multiply_fusion
  913.6 1.3 broadcast_multiply_fusion.1
  914.9 1.0 copy.44
  915.9 1.6 convert_element_type.28
  (21 shorter events, 0.1 us)
Async XLA Ops:
  7.2 41.6 %all-gather.4.cloned.1.call-start = ((), (), s32[]{:S(2)}) async-start(), calls=%async_computation.2 | async-start | bytes 2228224 | tf_op jit(solution)/shard_map/all_gather | solution.py:13
  7.9 126.8 %all-gather.6.cloned.1.call-start = ((), (), s32[]{:S(2)}) async-start(), calls=%async_computation.4 | async-start | bytes 2228224 | tf_op jit(solution)/shard_map/all_gather | solution.py:14
  8.6 904.9 %all-reduce.4.cloned.1.call-start = ((), (), s32[]{:S(2)}) async-start(), calls=%async_computation.3 | async-start | bytes 2048000 | tf_op jit(solution)/shard_map/psum | solution.py:63
  140.2 6.3 copy-start
  158.0 757.9 %reduce-scatter.4.cloned.1.call-start = ((), (), s32[]{:S(2)}) async-start(), calls=%async_computation.1 | async-start | bytes 4456448 | tf_op jit(solution)/shard_map/reduce_scatter | solution.py:49
  776.6 9.6 %collective-permute-start.15 = (f32[30,256]{1,0:T(8,128)S(1)}, f32[30,256]{1,0:T(8,128)S(1)}, u32[]{:S(2)}, u32[]{:S(2)}) collective-permute-start(f32[30,256]{1,0:T(8,128)S(1)} %slice.56), channel_id=1, source_target_pairs={{0,16},{1,17},{2,18},{3,19},{4,20},{5,21},{6,22},{7,23},{8,24},{9,... | collective-permute-start | bytes 92168
  778.6 14.5 %collective-permute-start.14 = (f32[32,256]{1,0:T(8,128)S(1)}, f32[32,256]{1,0:T(8,128)S(1)}, u32[]{:S(2)}, u32[]{:S(2)}) collective-permute-start(f32[32,256]{1,0:T(8,128)S(1)} %fusion), channel_id=1, source_target_pairs={{0,15},{1,16},{2,17},{3,18},{4,19},{5,20},{6,21},{7,22},{8,23},{9,... | collective-permute-start | bytes 98312
  780.5 20.6 %collective-permute-start.13 = (f32[32,256]{1,0:T(8,128)S(1)}, f32[32,256]{1,0:T(8,128)S(1)}, u32[]{:S(2)}, u32[]{:S(2)}) collective-permute-start(f32[32,256]{1,0:T(8,128)S(1)} %fusion), channel_id=1, source_target_pairs={{0,14},{1,15},{2,16},{3,17},{4,18},{5,19},{6,20},{7,21},{8,22},{9,... | collective-permute-start | bytes 98312
  782.4 20.6 %collective-permute-start.12 = (f32[32,256]{1,0:T(8,128)S(1)}, f32[32,256]{1,0:T(8,128)S(1)}, u32[]{:S(2)}, u32[]{:S(2)}) collective-permute-start(f32[32,256]{1,0:T(8,128)S(1)} %fusion), channel_id=1, source_target_pairs={{0,13},{1,14},{2,15},{3,16},{4,17},{5,18},{6,19},{7,20},{8,21},{9,... | collective-permute-start | bytes 98312
  784.3 33.6 %collective-permute-start.11 = (f32[32,256]{1,0:T(8,128)S(1)}, f32[32,256]{1,0:T(8,128)S(1)}, u32[]{:S(2)}, u32[]{:S(2)}) collective-permute-start(f32[32,256]{1,0:T(8,128)S(1)} %fusion), channel_id=1, source_target_pairs={{0,12},{1,13},{2,14},{3,15},{4,16},{5,17},{6,18},{7,19},{8,20},{9,... | collective-permute-start | bytes 98312
  786.3 59.5 %collective-permute-start.10 = (f32[32,256]{1,0:T(8,128)S(1)}, f32[32,256]{1,0:T(8,128)S(1)}, u32[]{:S(2)}, u32[]{:S(2)}) collective-permute-start(f32[32,256]{1,0:T(8,128)S(1)} %fusion), channel_id=1, source_target_pairs={{0,11},{1,12},{2,13},{3,14},{4,15},{5,16},{6,17},{7,18},{8,19},{9,... | collective-permute-start | bytes 98312
  793.0 77.1 %collective-permute-start.9 = (f32[32,256]{1,0:T(8,128)S(1)}, f32[32,256]{1,0:T(8,128)S(1)}, u32[]{:S(2)}, u32[]{:S(2)}) collective-permute-start(f32[32,256]{1,0:T(8,128)S(1)} %fusion), channel_id=1, source_target_pairs={{0,10},{1,11},{2,12},{3,13},{4,14},{5,15},{6,16},{7,17},{8,18},{9,... | collective-permute-start | bytes 98312
  801.1 86.0 %collective-permute-start.8 = (f32[32,256]{1,0:T(8,128)S(1)}, f32[32,256]{1,0:T(8,128)S(1)}, u32[]{:S(2)}, u32[]{:S(2)}) collective-permute-start(f32[32,256]{1,0:T(8,128)S(1)} %fusion), channel_id=1, source_target_pairs={{0,9},{1,10},{2,11},{3,12},{4,13},{5,14},{6,15},{7,16},{8,17},{9,1... | collective-permute-start | bytes 98312
  803.1 86.6 %collective-permute-start.7 = (f32[32,256]{1,0:T(8,128)S(1)}, f32[32,256]{1,0:T(8,128)S(1)}, u32[]{:S(2)}, u32[]{:S(2)}) collective-permute-start(f32[32,256]{1,0:T(8,128)S(1)} %fusion), channel_id=1, source_target_pairs={{0,8},{1,9},{2,10},{3,11},{4,12},{5,13},{6,14},{7,15},{8,16},{9,17... | collective-permute-start | bytes 98312
  817.9 80.4 %collective-permute-start.6 = (f32[32,256]{1,0:T(8,128)S(1)}, f32[32,256]{1,0:T(8,128)S(1)}, u32[]{:S(2)}, u32[]{:S(2)}) collective-permute-start(f32[32,256]{1,0:T(8,128)S(1)} %fusion), channel_id=1, source_target_pairs={{0,7},{1,8},{2,9},{3,10},{4,11},{5,12},{6,13},{7,14},{8,15},{9,16}... | collective-permute-start | bytes 98312
  845.8 55.6 %collective-permute-start.5 = (f32[32,256]{1,0:T(8,128)S(1)}, f32[32,256]{1,0:T(8,128)S(1)}, u32[]{:S(2)}, u32[]{:S(2)}) collective-permute-start(f32[32,256]{1,0:T(8,128)S(1)} %fusion), channel_id=1, source_target_pairs={{0,6},{1,7},{2,8},{3,9},{4,10},{5,11},{6,12},{7,13},{8,14},{9,15},... | collective-permute-start | bytes 98312
  870.1 33.2 %collective-permute-start.4 = (f32[32,256]{1,0:T(8,128)S(1)}, f32[32,256]{1,0:T(8,128)S(1)}, u32[]{:S(2)}, u32[]{:S(2)}) collective-permute-start(f32[32,256]{1,0:T(8,128)S(1)} %fusion), channel_id=1, source_target_pairs={{0,5},{1,6},{2,7},{3,8},{4,9},{5,10},{6,11},{7,12},{8,13},{9,14},{... | collective-permute-start | bytes 98312
  887.1 16.3 %collective-permute-start.3 = (f32[32,256]{1,0:T(8,128)S(1)}, f32[32,256]{1,0:T(8,128)S(1)}, u32[]{:S(2)}, u32[]{:S(2)}) collective-permute-start(f32[32,256]{1,0:T(8,128)S(1)} %fusion), channel_id=1, source_target_pairs={{0,4},{1,5},{2,6},{3,7},{4,8},{5,9},{6,10},{7,11},{8,12},{9,13},{1... | collective-permute-start | bytes 98312
  889.6 17.5 %collective-permute-start.2 = (f32[32,256]{1,0:T(8,128)S(1)}, f32[32,256]{1,0:T(8,128)S(1)}, u32[]{:S(2)}, u32[]{:S(2)}) collective-permute-start(f32[32,256]{1,0:T(8,128)S(1)} %fusion), channel_id=1, source_target_pairs={{0,3},{1,4},{2,5},{3,6},{4,7},{5,8},{6,9},{7,10},{8,11},{9,12},{10... | collective-permute-start | bytes 98312
  898.3 10.0 %collective-permute-start.1 = (f32[32,256]{1,0:T(8,128)S(1)}, f32[32,256]{1,0:T(8,128)S(1)}, u32[]{:S(2)}, u32[]{:S(2)}) collective-permute-start(f32[32,256]{1,0:T(8,128)S(1)} %fusion), channel_id=1, source_target_pairs={{0,2},{1,3},{2,4},{3,5},{4,6},{5,7},{6,8},{7,9},{8,10},{9,11},{10,... | collective-permute-start | bytes 98312
  901.4 9.5 %collective-permute-start = (f32[32,256]{1,0:T(8,128)S(1)}, f32[32,256]{1,0:T(8,128)S(1)}, u32[]{:S(2)}, u32[]{:S(2)}) collective-permute-start(f32[32,256]{1,0:T(8,128)S(1)} %fusion), channel_id=1, source_target_pairs={{0,1},{1,2},{2,3},{3,4},{4,5},{5,6},{6,7},{7,8},{8,9},{9,10},{10,1... | collective-permute-start | bytes 98312
Sparse Core Ops, SparseCore 0:
  9.8 38.8 all-gather.3
  51.3 83.2 all-gather.5
  158.1 258.4 all-reduce.3
  419.0 74.0 reduce-scatter.3
where the time goes:
time: 925 us; the launch traced here: 924 us
  blocking collectives  598 us (65%)
  starting transfers between devices  127 us (14%)
  waiting for transfers between devices  120 us (13%)
  other arithmetic  27.4 us (3%)
  local copies, waits for them, and re-layouts  20.9 us (2%)
  matrix products  17.1 us (2%)
  between operations  14.1 us (2%)
    unnamed x1, blocking collectives  598 us
    unnamed x16, starting transfers between devices  126 us
    all_gather x1, waiting for transfers between devices, on_device(): target_rows = lax.all_gather(dest_grad[0], 'row', axis=0, tiled=True)  80.1 us
    all_gather x1, waiting for transfers between devices, on_device(): source_rows = lax.all_gather(node_feats, 'col', axis=0, tiled=True)  31.2 us
  transfers between devices with their start and end apart: 20, of which 5 were waited for; matrix products, arithmetic and copies ran while one was open for 69% of the time, Pallas kernels for 0%

commit v1 on v0

v1 whole, which is shorter than its diff:
```python
import functools

import jax
import jax.numpy as jnp
from jax import lax
from jax.experimental import pallas as pl
from jax.experimental.pallas import tpu as pltpu
from jax.sharding import PartitionSpec as P

MESH = pl.DeviceIdType.MESH
BF16 = jnp.bfloat16
F32 = jnp.float32
D = 256
BASES = 30
RELS = 2000
EDGES = 1024
EDGE_BLOCK = 128
VMEM = pltpu.VMEM


class Place:
    def __init__(self):
        i, j = lax.axis_index("row"), lax.axis_index("col")
        self.i, self.j = i, j
        self.z, self.xh = lax.rem(i, 8), lax.div(i, 8)
        self.y, self.xl, self.c = lax.div(j, 4), lax.rem(lax.div(j, 2), 2), lax.rem(j, 2)
        self.x = self.xh * 2 + self.xl

    def at(self, z=None, y=None, x=None, c=None):
        z = self.z if z is None else z
        y = self.y if y is None else y
        x = self.x if x is None else x
        c = self.c if c is None else c
        return (lax.div(x, 2) * 8 + z, y * 4 + lax.rem(x, 2) * 2 + c)


def wrap(value, n):
    return lax.rem(value + 2 * n, n)


def greet(peers):
    barrier = pltpu.get_barrier_semaphore()
    for peer in peers:
        pl.semaphore_signal(barrier, inc=1, device_id=peer, device_id_type=MESH)
    pl.semaphore_wait(barrier, len(peers))


class Mail:
    def __init__(self, send_sems, recv_sems):
        self.send_sems, self.recv_sems, self.count, self.sent = send_sems, recv_sems, 0, []

    def send(self, src, dst, peer):
        copy = pltpu.make_async_remote_copy(
            src_ref=src,
            dst_ref=dst,
            send_sem=self.send_sems.at[self.count],
            recv_sem=self.recv_sems.at[self.count],
            device_id=peer,
            device_id_type=MESH,
        )
        self.count += 1
        copy.start()
        self.sent.append(copy)
        return copy

    def finish(self):
        for copy in self.sent:
            copy.wait_send()


GATHER_MESSAGES = 40


def gather_kernel(
    fill, nf, dg, src, dst, rel, norm, coefs, xt_out, gt_out, ct_out,
    nbuf, dbuf, xacc, gacc, send_sems, recv_sems,
):
    me = Place()
    mail = Mail(send_sems, recv_sems)
    zup, zdn = me.at(z=wrap(me.z + 1, 8)), me.at(z=wrap(me.z - 1, 8))
    yup, ydn = me.at(y=wrap(me.y + 1, 4)), me.at(y=wrap(me.y - 1, 4))
    xnear = me.at(x=me.xh * 2 + 1 - me.xl)
    xfar = me.at(x=(1 - me.xh) * 2 + me.xl)
    sib = me.at(c=1 - me.c)
    greet([zup, zdn, yup, ydn, xnear, xfar, sib])

    def drow(q, z):
        return (me.xh if q == 0 else 1 - me.xh) * 8 + wrap(z, 8)

    def ncol(q, y, c):
        return wrap(y, 4) * 4 + (me.xl if q == 0 else 1 - me.xl) * 2 + c

    def dsend(q, d, up):
        sign = -1 if up else 1
        slot = drow(q, me.z + sign * d)
        peer = zup if up else zdn
        if d == 0 and q == 0:
            return mail.send(dg, dbuf.at[slot], peer)
        if d < 3:
            return mail.send(dbuf.at[slot], dbuf.at[slot], peer)
        half = pl.ds(0, 128) if up else pl.ds(128, 128)
        return mail.send(dbuf.at[slot, half], dbuf.at[slot, half], peer)

    def nsend(q, d, up):
        sign = -1 if up else 1
        slot = ncol(q, me.y + sign * d, me.c)
        peer = yup if up else ydn
        if d == 0 and q == 0:
            return mail.send(nf, nbuf.at[slot], peer)
        if d == 0:
            return mail.send(nbuf.at[slot], nbuf.at[slot], peer)
        half = pl.ds(0, 128) if up else pl.ds(128, 128)
        return mail.send(nbuf.at[slot, half], nbuf.at[slot, half], peer)

    def pass_on(slot):
        return mail.send(nbuf.at[slot], nbuf.at[slot], sib)

    vertex = lax.broadcasted_iota(jnp.int32, (256, EDGES), 0)

    def select(ids, base, rows, acc, first=False):
        hot = jnp.where(vertex + base == ids[...], 1.0, 0.0).astype(BF16)
        picked = lax.dot_general(
            rows, hot, (((0,), (0,)), ((), ())), preferred_element_type=F32
        )
        if first:
            acc[...] = picked
        else:
            acc[...] += picked

    def take_d(slot):
        select(dst, slot * 256, dbuf[slot], gacc)

    def take_n(slot):
        select(src, slot * 256, nbuf[slot], xacc)

    d = {}
    n = {}
    d[0, 0, 1], d[0, 0, 0] = dsend(0, 0, True), dsend(0, 0, False)
    far = mail.send(dg, dbuf.at[drow(0, me.z)], xfar)
    near = mail.send(nf, nbuf.at[ncol(0, me.y, me.c)], xnear)
    n[0, 0, 1], n[0, 0, 0] = nsend(0, 0, True), nsend(0, 0, False)
    own = mail.send(nf, nbuf.at[ncol(0, me.y, me.c)], sib)

    select(dst, me.i * 256, dg[...], gacc, first=True)
    select(src, me.j * 256, nf[...], xacc, first=True)

    for up in (1, 0):
        d[0, 0, up].wait_recv()
        d[0, 1, up] = dsend(0, 1, bool(up))
    far.wait_recv()
    for up in (1, 0):
        d[1, 0, up] = dsend(1, 0, bool(up))
    near.wait_recv()
    for up in (1, 0):
        n[1, 0, up] = nsend(1, 0, bool(up))
    passed = {(1, 0): pass_on(ncol(1, me.y, me.c))}
    for up in (1, 0):
        n[0, 0, up].wait_recv()
        n[0, 1, up] = nsend(0, 1, bool(up))
        passed[0, up] = pass_on(ncol(0, me.y + (-1 if up else 1), me.c))

    for start in range(0, RELS, 256):
        size = min(256, RELS - start)
        relation = lax.broadcasted_iota(jnp.int32, (size, EDGES), 0) + start
        hot = jnp.where(relation == rel[...], 1.0, 0.0).astype(BF16)
        part = lax.dot_general(
            coefs[start : start + size, :], hot, (((0,), (0,)), ((), ())),
            preferred_element_type=F32,
        )
        if start == 0:
            ct_out[0:BASES, :] = part
        else:
            ct_out[0:BASES, :] += part
    ct_out[BASES:32, :] = jnp.zeros((2, EDGES), F32)

    def arrive_d(q, dist, forward):
        for up in (1, 0):
            d[q, dist, up].wait_recv()
            if forward:
                d[q, dist + 1, up] = dsend(q, dist + 1, bool(up))

    def both_d(q, dist):
        take_d(drow(q, me.z - dist))
        take_d(drow(q, me.z + dist))

    arrive_d(0, 1, True)
    both_d(0, 1)
    take_d(drow(1, me.z))
    take_n(ncol(1, me.y, me.c))
    arrive_d(1, 0, True)
    for up in (1, 0):
        n[1, 0, up].wait_recv()
        n[1, 1, up] = nsend(1, 1, bool(up))
        passed[1, 2 + up] = pass_on(ncol(1, me.y + (-1 if up else 1), me.c))
    own.wait_recv()
    take_n(ncol(0, me.y - 1, me.c))
    take_n(ncol(0, me.y + 1, me.c))
    take_n(ncol(0, me.y, 1 - me.c))
    both_d(1, 1)
    arrive_d(0, 2, True)
    for up in (1, 0):
        n[0, 1, up].wait_recv()
    passed[0, 2] = pass_on(ncol(0, me.y + 2, me.c))
    both_d(0, 2)
    take_n(ncol(0, me.y + 2, me.c))
    take_n(ncol(1, me.y + 1, me.c))
    take_n(ncol(1, me.y - 1, me.c))
    arrive_d(1, 1, True)
    for up in (1, 0):
        n[1, 1, up].wait_recv()
    passed[1, 4] = pass_on(ncol(1, me.y + 2, me.c))
    take_n(ncol(1, me.y + 2, me.c))
    for key in passed:
        passed[key].wait_recv()
    for q, y in ((1, me.y), (0, me.y - 1), (0, me.y + 1), (1, me.y - 1), (1, me.y + 1), (0, me.y + 2), (1, me.y + 2)):
        take_n(ncol(q, y, 1 - me.c))
    xt_out[...] = xacc[...].astype(BF16)
    arrive_d(0, 3, False)
    both_d(0, 3)
    take_d(drow(0, me.z + 4))
    arrive_d(1, 2, True)
    both_d(1, 2)
    both_d(1, 3)
    arrive_d(1, 3, False)
    take_d(drow(1, me.z + 4))

    lane = lax.broadcasted_iota(jnp.int32, (1, EDGE_BLOCK), 1)
    for block in range(EDGES // EDGE_BLOCK):
        lanes = pl.ds(block * EDGE_BLOCK, EDGE_BLOCK)
        weight = norm[:, lanes] * jnp.where(lane < fill[0, block], 1.0, 0.0).astype(F32)
        gt_out[:, lanes] = (gacc[:, lanes] * weight).astype(BF16)
    mail.finish()


def compute_kernel(
    xt, gt, ct, src, rel, bases, npart, bpart, grads, xf, per_edge, inner, coef_part, basis_part
):
    grads[...] = gt[...].T
    xf[...] = xt[...].astype(F32)
    per_edge[...] = jnp.zeros_like(per_edge)
    inner[BASES:32, :] = jnp.zeros((2, EDGES), F32)

    @pl.loop(0, BASES)
    def _(b):
        coef = ct[pl.ds(b, 1), :]
        backed = jnp.dot(bases[b], gt[...], preferred_element_type=F32)
        per_edge[...] += coef * backed
        inner[pl.ds(b, 1), :] = jnp.sum(backed * xf[...], axis=0, keepdims=True)
        scaled = (coef * xf[...]).astype(BF16)
        start = pl.multiple_of(b * D, D)
        basis_part[pl.ds(start, D), :] = jnp.dot(scaled, grads[...], preferred_element_type=F32)

    values = per_edge[...].T.astype(BF16)
    vertex = lax.broadcasted_iota(jnp.int32, (256, EDGES), 0)

    @pl.loop(0, 16)
    def _(block):
        hot = jnp.where(vertex + block * 256 == src[...], 1.0, 0.0).astype(BF16)
        slot = lax.rem(block, 2) * 8 + lax.div(block, 2)
        npart[slot] = jnp.dot(hot, values, preferred_element_type=F32).astype(BF16)

    high = inner[...].astype(BF16)
    low = (inner[...] - high.astype(F32)).astype(BF16)
    both = jnp.concatenate([high, low], axis=0)
    for block in range(8):
        hot = jnp.where(vertex + block * 256 == rel[...], 1.0, 0.0).astype(BF16)
        part = lax.dot_general(both, hot, (((1,), (1,)), ((), ())), preferred_element_type=F32)
        coef_part[:, block, :] = part[0:32] + part[32:64]

    @pl.loop(0, 32)
    def _(group):
        rows = basis_part[pl.ds(pl.multiple_of(group * 240, 8), 240), :]
        extra = coef_part[group]
        row = lax.div(group, 2)
        z, xh = lax.rem(row, 8), lax.div(row, 8)
        for u in range(8):
            y = lax.rem(2 * group + u // 4, 4)
            xl, c = (u % 4) // 2, u % 2
            slot = c * 128 + z * 16 + y * 4 + xh * 2 + xl
            piece = jnp.concatenate(
                [rows[30 * u : 30 * u + 30], extra[u : u + 1], jnp.zeros((1, D), F32)], axis=0
            ).astype(BF16)
            bpart[2 * slot] = piece[0:16]
            bpart[2 * slot + 1] = piece[16:32]


def ring_steps(mail, acc, base, unit, n, p, up, down, heads, bodies):
    half = unit // 2
    start = lambda q: base + wrap(q, n) * unit
    opposite = start(p + n // 2)
    flights = [
        mail.send(acc.at[pl.ds(opposite, half)], heads.at[0], up),
        mail.send(acc.at[pl.ds(opposite + half, half)], heads.at[1], down),
    ]
    for step in range(1, n // 2):
        following = []
        for way, peer in ((0, up), (1, down)):
            first = start(p + (n // 2 - step) * (1 if way == 0 else -1))
            yield
            flights[way].wait_recv()
            if step == 1:
                add_into(acc, first + way * half, half, [heads.at[way]])
            else:
                add_into(acc, first, unit, [bodies.at[way, step - 2]])
            following.append(mail.send(acc.at[pl.ds(first, unit)], bodies.at[way, step - 1], peer))
        flights = following
    yield
    for flight in flights:
        flight.wait_recv()
    last = n // 2 - 2
    add_into(acc, start(p), unit, [bodies.at[0, last], bodies.at[1, last]])


def add_into(acc, first, count, sources):
    def body(k, carry):
        total = acc[first + k].astype(F32)
        for source in sources:
            total = total + source[k].astype(F32)
        acc[first + k] = total.astype(BF16)
        return carry

    if count == 1:
        body(0, 0)
    else:
        lax.fori_loop(0, count, body, 0)


def run(*streams):
    streams = list(streams)
    while streams:
        for stream in list(streams):
            try:
                next(stream)
            except StopIteration:
                streams.remove(stream)


REDUCE_MESSAGES = 70


def reduce_kernel(
    npart, bpart, node_out, basis_out, coef_out,
    nfrom, nacc, nheads, nbodies, nnear, bfrom, bacc, zheads, zbodies, yheads, ybodies, xheads, xbodies,
    send_sems, recv_sems,
):
    me = Place()
    mail = Mail(send_sems, recv_sems)
    zup, zdn = me.at(z=wrap(me.z + 1, 8)), me.at(z=wrap(me.z - 1, 8))
    yup, ydn = me.at(y=wrap(me.y + 1, 4)), me.at(y=wrap(me.y - 1, 4))
    xup, xdn = me.at(x=wrap(me.x + 1, 4)), me.at(x=wrap(me.x - 1, 4))
    xnear = me.at(x=me.xh * 2 + 1 - me.xl)
    sib = me.at(c=1 - me.c)
    row_peers = [(wrap(me.i + k, 16), me.j) for k in range(1, 16)]
    col_peers = [(me.i, wrap(me.j + k, 16)) for k in range(1, 16)]
    greet(row_peers + col_peers + [xup, xdn])

    node_core = mail.send(npart.at[pl.ds((1 - me.c) * 8, 8)], nfrom, sib)
    basis_core = mail.send(bpart.at[pl.ds((1 - me.c) * 256, 256)], bfrom, sib)

    def node_stream():
        node_core.wait_recv()

        def body(k, carry):
            nacc[k] = (npart[me.c * 8 + k].astype(F32) + nfrom[k].astype(F32)).astype(BF16)
            return carry

        lax.fori_loop(0, 8, body, 0)
        yield from ring_steps(mail, nacc, 0, 2, 4, me.y, yup, ydn, nheads, nbodies)
        near = mail.send(nacc.at[me.y * 2 + 1 - me.xl], nnear, xnear)
        yield
        near.wait_recv()
        node_out[...] = (nacc[me.y * 2 + me.xl].astype(F32) + nnear[...].astype(F32)).astype(BF16)

    def basis_stream():
        basis_core.wait_recv()

        def body(k, carry):
            bacc[k] = (bpart[me.c * 256 + k].astype(F32) + bfrom[k].astype(F32)).astype(BF16)
            return carry

        lax.fori_loop(0, 256, body, 0)
        yield from ring_steps(mail, bacc, 0, 32, 8, me.z, zup, zdn, zheads, zbodies)
        base = me.z * 32
        yield from ring_steps(mail, bacc, base, 8, 4, me.y, yup, ydn, yheads, ybodies)
        base = base + me.y * 8
        yield from ring_steps(mail, bacc, base, 2, 4, me.x, xup, xdn, xheads, xbodies)
        base = base + me.x * 2
        total = jnp.concatenate([bacc[base].astype(F32), bacc[base + 1].astype(F32)], axis=0) * (1.0 / 16)
        basis_out[...] = total[0:BASES]
        mine = me.i * 16 + me.j
        coef_out[mine] = total[BASES : BASES + 1]
        flights = [mail.send(coef_out.at[mine], coef_out.at[mine], peer) for peer in col_peers]
        yield
        for flight in flights:
            flight.wait_recv()
        group = pl.ds(me.i * 16, 16)
        flights = [mail.send(coef_out.at[group], coef_out.at[group], peer) for peer in row_peers]
        yield
        for flight in flights:
            flight.wait_recv()

    run(node_stream(), basis_stream())
    mail.finish()


def on_device(
    node_feats, dest_grad, bases, coefs, src_ids, dst_ids, rel_ids, edge_norm, block_fill
):
    src, dst, rel = (a.reshape(1, EDGES) for a in (src_ids, dst_ids, rel_ids))
    norm = edge_norm.reshape(1, EDGES)
    vm = pl.BlockSpec(memory_space=VMEM)
    xt, gt, ct = pl.pallas_call(
        gather_kernel,
        out_shape=(
            jax.ShapeDtypeStruct((D, EDGES), BF16),
            jax.ShapeDtypeStruct((D, EDGES), BF16),
            jax.ShapeDtypeStruct((32, EDGES), F32),
        ),
        in_specs=[pl.BlockSpec(memory_space=pltpu.SMEM)] + [vm] * 7,
        out_specs=(vm, vm, vm),
        scratch_shapes=[
            VMEM((16, 256, D), BF16),
            VMEM((16, 256, D), BF16),
            VMEM((D, EDGES), F32),
            VMEM((D, EDGES), F32),
            pltpu.SemaphoreType.DMA((GATHER_MESSAGES,)),
            pltpu.SemaphoreType.DMA((GATHER_MESSAGES,)),
        ],
        compiler_params=pltpu.CompilerParams(collective_id=0, has_side_effects=True),
    )(block_fill.reshape(1, 8), node_feats, dest_grad[0], src, dst, rel, norm, coefs)
    npart, bpart = pl.pallas_call(
        compute_kernel,
        out_shape=(
            jax.ShapeDtypeStruct((16, 256, D), BF16),
            jax.ShapeDtypeStruct((512, 16, D), BF16),
        ),
        in_specs=[vm] * 6,
        out_specs=(vm, vm),
        scratch_shapes=[
            VMEM((EDGES, D), BF16),
            VMEM((D, EDGES), F32),
            VMEM((D, EDGES), F32),
            VMEM((32, EDGES), F32),
            VMEM((32, 8, D), F32),
            VMEM((BASES * D, D), F32),
        ],
    )(xt, gt, ct, src, rel, bases)
    dma = pltpu.SemaphoreType.DMA((REDUCE_MESSAGES,))
    node_grad, basis_grad, coef_rows = pl.pallas_call(
        reduce_kernel,
        out_shape=(
            jax.ShapeDtypeStruct((256, D), BF16),
            jax.ShapeDtypeStruct((BASES, D), F32),
            jax.ShapeDtypeStruct((256, 1, D), F32),
        ),
        in_specs=[vm] * 2,
        out_specs=(vm, vm, vm),
        scratch_shapes=[
            VMEM((8, 256, D), BF16),
            VMEM((8, 256, D), BF16),
            VMEM((2, 1, 256, D), BF16),
            VMEM((2, 1, 2, 256, D), BF16),
            VMEM((256, D), BF16),
            VMEM((256, 16, D), BF16),
            VMEM((256, 16, D), BF16),
            VMEM((2, 16, 16, D), BF16),
            VMEM((2, 3, 32, 16, D), BF16),
            VMEM((2, 4, 16, D), BF16),
            VMEM((2, 1, 8, 16, D), BF16),
            VMEM((2, 1, 16, D), BF16),
            VMEM((2, 1, 2, 16, D), BF16),
            dma,
            dma,
        ],
        compiler_params=pltpu.CompilerParams(collective_id=1, has_side_effects=True),
    )(npart, bpart)
    coef_grad = coef_rows.reshape(32, 2048)[:BASES, :RELS].T
    return node_grad, basis_grad, coef_grad


def solution(mesh):
    in_specs = (
        P(("row", "col"), None),
        P("col", "row", None),
        P(),
        P(),
        P("row", "col", None),
        P("row", "col", None),
        P("row", "col", None),
        P("row", "col", None),
        P("row", "col", None),
    )
    out_specs = (P(("row", "col"), None), P(("row", "col"), None), P())
    return jax.shard_map(
        on_device, mesh=mesh, in_specs=in_specs, out_specs=out_specs, check_vma=False
    )
```

time: 925 us -> 148 us (0.16)
  the two profiles are of different devices: /device:TPU:4 before, /device:TPU:1 now
where the time goes in v1:
time: 148 us
  Pallas kernels  140 us (95%)
  local copies, waits for them, and re-layouts  5.66 us (4%)
  other arithmetic  1.57 us (1%)
    pallas_call x1, Pallas kernels, on_device(): pl.pallas_call(reduce_kernel, out_shape=(jax.ShapeDtypeStruct((256, D), B...  75.6 us
    pallas_call x1, Pallas kernels, on_device(): pl.pallas_call(gather_kernel, out_shape=(jax.ShapeDtypeStruct((D, EDGES),...  36.5 us
    pallas_call x1, Pallas kernels, on_device(): pl.pallas_call(compute_kernel, out_shape=(jax.ShapeDtypeStruct((16, 256,...  27.5 us
    unnamed x3, local copies, waits for them, and re-layouts  4.89 us

profile of v1, /device:TPU:1, one launch (start us, length us, event | category | flops | bytes accessed | tf_op | source)
XLA Modules:
  0.0 147.6 jit_solution(13065152451950478943)
XLA Ops:
  0.6 2.0 %copy.12.coefs = bf16[2000,30]{1,0:T(8,128)(2,1)} copy(bf16[2000,30]{0,1:T(8,128)(2,1)} %param.12) | data formatting | bytes 240000 | tf_op args[3]
  2.6 36.5 %shard_map.112 = (bf16[256,1024]{1,0:T(8,128)(2,1)}, bf16[256,1024]{1,0:T(8,128)(2,1)}, f32[32,1024]{1,0:T(8,128)}) custom-call(s32[1,8]{1,0:T(1,128)} %bitcast.15, bf16[256,256]{1,0:T(8,128)(2,1)} %nf.1, bf16[256,256]{1,0:T(8,128)(2,1)} %bitcast.8, s32[1,1024]{1,0:T(1,128)} %bitcast.9, s32[1,1024]{1,0:T(1,128)} %bitcast.13, s32[1,1024]{1,0:T(1,128)} %bitcast.11, ...), custom_call_target="tpu_custom_call" | custom-call | tf_op jit(solution)/shard_map/pallas_call | solution.py:412
  39.1 27.5 %shard_map.113 = (bf16[16,256,256]{2,1,0:T(8,128)(2,1)}, bf16[512,16,256]{2,1,0:T(8,128)(2,1)}) custom-call(bf16[256,1024]{1,0:T(8,128)(2,1)} %get-tuple-element.11.xt, bf16[256,1024]{1,0:T(8,128)(2,1)} %get-tuple-element.12.gt, f32[32,1024]{1,0:T(8,128)} %get-tuple-element.13.ct, s32[1,1024]{1,0:T(1,128)} %bitcast.10, s32[1,1024]{1,0:T(1,128)} %bitcast.12, ...), custom_call_target="tpu_custom_call" | custom-call | tf_op jit(solution)/shard_map/pallas_call | solution.py:431
  66.6 75.6 %shard_map.114 = (bf16[256,256]{1,0:T(8,128)(2,1)}, f32[30,256]{1,0:T(8,128)}, f32[256,1,256]{2,1,0:T(1,128)}) custom-call(bf16[16,256,256]{2,1,0:T(8,128)(2,1)} %get-tuple-element.14.npart, bf16[512,16,256]{2,1,0:T(8,128)(2,1)} %get-tuple-element.15.bpart), custom_call_target="tpu_custom_call" | custom-call | tf_op jit(solution)/shard_map/pallas_call | solution.py:449
  142.3 1.6 %reduce = f32[256,256]{1,0:T(8,128)S(1)} reduce(f32[256,1,256]{2,1,0:T(1,128)} %get-tuple-element.18, f32[]{:T(128)} %constant.6), dimensions={1}, to_apply=%get-tuple-element.18.reduce_sub_computation | reduce | bytes 524292 | tf_op jit(solution)/shard_map/pallas_call | solution.py:449
  143.9 0.7 slice_bitcast_fusion
  144.6 1.6 %copy.15 = bf16[256,256]{1,0:T(8,128)(2,1)} copy(bf16[256,256]{1,0:T(8,128)(2,1)} %get-tuple-element.22) | data formatting | bytes 262144
  146.2 1.4 copy.16
  (1 shorter events, 0.0 us)
